TPU v7x, 128 devices: a whole 4x4x4 slice. The times are simulated.
128 devices in a mesh: seg: 8 (over y_lo, z), grp: 16 (over x, y_hi, core).
Axes of the slice: x: 4, y: 4 (y_hi: 2, y_lo: 2; y = y_hi * 2 + y_lo), z: 4, core: 2. Of those that a mesh axis runs over, the one named last changes fastest.
Arguments:
- frames_in: bfloat16 [128, 32, 120, 128], P(('seg', 'grp')), may hold values from -6 to 6
- spatial_weight: bfloat16 [9, 128, 128], replicated, may hold values from -0.1875 to 0.1875
- temporal_weight: bfloat16 [2, 5, 128, 128], replicated, may hold values from -0.25 to 0.25
- uniting_weight: bfloat16 [2, 128, 128], replicated, may hold values from -0.375 to 0.375
- key_index: int32 [8], replicated, may hold values from 0 to 15
- dilation: int32 [2], replicated, may hold values from 1 to 8, as said below
- cotangent: bfloat16 [128, 32, 120, 128], P(('seg', 'grp')), may hold values from -6 to 6
Outputs:
- united: bfloat16 [128, 32, 120, 128], P(('seg', 'grp'))
- grad_frames: bfloat16 [128, 32, 120, 128], P(('seg', 'grp'))
- grad_spatial: float32 [9, 128, 128], replicated
- grad_temporal: float32 [2, 5, 128, 128], replicated
- grad_uniting: float32 [2, 128, 128], replicated
Inputs may be any that keep to these rules, and one draw needn't show every extreme that they name: `key_index`: position of a segment's keyframe within its 16 frames. Exactly one layer uses dilation 8; the others use less.
All inputs are finite; a program needn't handle non-finite values.
Results may differ from a plain program's by a relative error of at most 0.0095.
Values may be sent and summed in bfloat16 or wider, within the bound.
A program may use at most 128 MiB of HBM per device.

v0:
```python
import jax
import jax.numpy as jnp
from jax import lax
from jax.sharding import PartitionSpec as P

LAYERS = 2
DMAX = 8


def from_root(value, axis, root):
    mine = lax.axis_index(axis) == root
    return lax.psum(jnp.where(mine, value, jnp.zeros_like(value)), axis)


def silu_grad(value):
    sigma = jax.nn.sigmoid(value)
    return sigma * (1.0 + value * (1.0 - sigma))


def inner(left, right):
    return lax.dot_general(
        left, right, (((0,), (0,)), ((), ())), preferred_element_type=jnp.float32
    )


def spatial_forward(frames, kernel):
    count, rows, cols, chans = frames.shape
    padded = jnp.pad(frames, ((0, 0), (1, 1), (1, 1), (0, 0)))
    total = jnp.zeros((count * rows * cols, chans), jnp.float32)
    for row_tap in range(3):
        for col_tap in range(3):
            piece = padded[:, row_tap : row_tap + rows, col_tap : col_tap + cols, :].reshape(
                -1, chans
            )
            total = total + jnp.dot(
                piece, kernel[3 * row_tap + col_tap], preferred_element_type=jnp.float32
            )
    return total.reshape(frames.shape)


def spatial_back(grads, kernel):
    count, rows, cols, chans = grads.shape
    padded = jnp.pad(grads, ((0, 0), (1, 1), (1, 1), (0, 0)))
    total = jnp.zeros((count * rows * cols, chans), jnp.float32)
    for row_tap in range(3):
        for col_tap in range(3):
            piece = padded[
                :, 2 - row_tap : 2 - row_tap + rows, 2 - col_tap : 2 - col_tap + cols, :
            ].reshape(-1, chans)
            total = total + jnp.dot(
                piece, kernel[3 * row_tap + col_tap].T, preferred_element_type=jnp.float32
            )
    return total.reshape(grads.shape)


def spatial_wgrad(frames, grads):
    count, rows, cols, chans = frames.shape
    padded = jnp.pad(frames, ((0, 0), (1, 1), (1, 1), (0, 0)))
    flat_grads = grads.reshape(-1, chans)
    result = []
    for row_tap in range(3):
        for col_tap in range(3):
            piece = padded[:, row_tap : row_tap + rows, col_tap : col_tap + cols, :].reshape(
                -1, chans
            )
            result.append(inner(piece, flat_grads))
    return jnp.stack(result)


def shifted(values, offset):
    padded = jnp.pad(values, ((2 * DMAX, 2 * DMAX), (0, 0), (0, 0)))
    start = 2 * DMAX + offset
    return lax.dynamic_slice_in_dim(padded, start, values.shape[0], 0)


def temporal_forward(acts, kernel, step_size):
    chans = acts.shape[2]
    total = jnp.zeros((acts.shape[0] * acts.shape[1], chans), jnp.float32)
    for tap in range(5):
        piece = shifted(acts, (tap - 2) * step_size).reshape(-1, chans)
        total = total + jnp.dot(piece, kernel[tap], preferred_element_type=jnp.float32)
    return total.reshape(acts.shape)


def temporal_back(grads, kernel, step_size):
    chans = grads.shape[2]
    total = jnp.zeros((grads.shape[0] * grads.shape[1], chans), jnp.float32)
    for tap in range(5):
        piece = shifted(grads, (2 - tap) * step_size).reshape(-1, chans)
        total = total + jnp.dot(piece, kernel[tap].T, preferred_element_type=jnp.float32)
    return total.reshape(grads.shape)


def temporal_wgrad(acts, grads, step_size):
    chans = acts.shape[2]
    flat_grads = grads.reshape(-1, chans)
    return jnp.stack(
        [
            inner(shifted(acts, (tap - 2) * step_size).reshape(-1, chans), flat_grads)
            for tap in range(5)
        ]
    )


def to_pixels(flat):
    return lax.all_to_all(flat, ("seg", "grp"), split_axis=1, concat_axis=0, tiled=True)


def to_frames(blocks):
    return lax.all_to_all(blocks, ("seg", "grp"), split_axis=0, concat_axis=1, tiled=True)


def local(
    frames_in, spatial_weight, temporal_weight, uniting_weight, key_index, dilation, cotangent
):
    local_frames, rows, cols, chans = frames_in.shape
    pixels = rows * cols
    seg_count = lax.axis_size("seg")
    pre_spatial = spatial_forward(frames_in, spatial_weight)
    act_zero = jax.nn.silu(pre_spatial).astype(jnp.bfloat16).reshape(local_frames, pixels, chans)
    cot_local = cotangent.reshape(local_frames, pixels, chans)
    act_blocks = to_pixels(act_zero)
    cot_blocks = lax.all_to_all(cot_local, ("seg", "grp"), split_axis=1, concat_axis=0, tiled=True)
    acts = [act_blocks]
    total_frames = acts[0].shape[0]
    block = acts[0].shape[1]
    seg_frames = total_frames // seg_count
    pres = []
    for layer in range(LAYERS):
        pre = temporal_forward(acts[-1], temporal_weight[layer], dilation[layer])
        pres.append(pre)
        acts.append(jax.nn.silu(pre).astype(jnp.bfloat16))
    feat = acts[-1]
    feat_seg = feat.reshape(seg_count, seg_frames, block, chans)
    positions = jnp.arange(seg_frames, dtype=jnp.int32)
    onehot = positions[None, :] == key_index[:, None]
    keys = jnp.einsum(
        "ns,nspc->npc", onehot.astype(jnp.bfloat16), feat_seg, preferred_element_type=jnp.float32
    ).astype(jnp.bfloat16)
    key_full = jnp.broadcast_to(keys[:, None], feat_seg.shape).reshape(-1, chans)
    feat_flat = feat.reshape(-1, chans)
    feat_time = to_frames(feat)
    seg_here = key_index[lax.axis_index("seg")]
    owner = seg_here // local_frames
    local_pos = seg_here % local_frames
    panel = lax.dynamic_index_in_dim(feat_time, local_pos, 0, keepdims=False)
    key_panel = from_root(panel, "grp", owner)
    key_part = jnp.dot(key_panel, uniting_weight[1], preferred_element_type=jnp.float32)
    main_part = jnp.dot(
        feat_time.reshape(-1, chans), uniting_weight[0], preferred_element_type=jnp.float32
    )
    united = (main_part.reshape(local_frames, pixels, chans) + key_part[None]).astype(jnp.bfloat16)
    cot_flat = cot_blocks.reshape(-1, chans)
    grad_feat = jnp.dot(cot_flat, uniting_weight[0].T, preferred_element_type=jnp.float32)
    seg_cot = jnp.sum(
        cot_blocks.reshape(seg_count, seg_frames, block, chans).astype(jnp.float32), axis=1
    )
    key_term = jnp.dot(
        seg_cot.reshape(-1, chans),
        uniting_weight[1].T.astype(jnp.float32),
        precision=lax.Precision.HIGHEST,
    ).reshape(seg_count, 1, block, chans)
    placed = onehot.astype(jnp.float32)[:, :, None, None] * key_term
    grad_feat = grad_feat.reshape(seg_count, seg_frames, block, chans) + placed
    grad_feat = grad_feat.reshape(total_frames, block, chans)
    grad_uniting = jnp.stack([inner(feat_flat, cot_flat), inner(key_full, cot_flat)])
    grad_pre = (grad_feat * silu_grad(pres[-1])).astype(jnp.bfloat16)
    tgrads = [None] * LAYERS
    grad_act0 = None
    for layer in range(LAYERS - 1, -1, -1):
        tgrads[layer] = temporal_wgrad(acts[layer], grad_pre, dilation[layer])
        grad_act = temporal_back(grad_pre, temporal_weight[layer], dilation[layer])
        if layer > 0:
            grad_pre = (grad_act * silu_grad(pres[layer - 1])).astype(jnp.bfloat16)
        else:
            grad_act0 = grad_act.astype(jnp.bfloat16)
    grad_time = to_frames(grad_act0).reshape(frames_in.shape)
    grad_spre = (grad_time.astype(jnp.float32) * silu_grad(pre_spatial)).astype(jnp.bfloat16)
    grad_frames = spatial_back(grad_spre, spatial_weight).astype(jnp.bfloat16)
    grad_spatial = spatial_wgrad(frames_in, grad_spre)
    summed = lax.psum((grad_spatial, jnp.stack(tgrads), grad_uniting), ("seg", "grp"))
    scale = 1.0 / jnp.sqrt(jnp.float32(total_frames * pixels))
    return (
        united.reshape(frames_in.shape),
        grad_frames,
        summed[0] * scale,
        summed[1] * scale,
        summed[2] * scale,
    )


def solution(mesh):
    placed = (
        P(("seg", "grp"), None, None, None),
        P(),
        P(),
        P(),
        P(),
        P(),
        P(("seg", "grp"), None, None, None),
    )
    return jax.shard_map(
        local,
        mesh=mesh,
        in_specs=placed,
        out_specs=(
            P(("seg", "grp"), None, None, None),
            P(("seg", "grp"), None, None, None),
            P(),
            P(),
            P(),
        ),
        check_vma=False,
    )
```

profile of v0, /device:TPU:0, one launch (start us, length us, event | category | flops | bytes accessed | tf_op | source)
XLA Modules:
  0.0 697.2 jit_solution(8917479555947847527)
XLA Ops:
  7.2 7.2 %pad_slice_fusion.8 = (bf16[1,32,120,128]{3,2,1,0:T(8,128)(2,1)S(1)}, bf16[1,32,120,128]{3,2,1,0:T(8,128)(2,1)S(1)}, bf16[1,32,120,128]{3,2,1,0:T(8,128)(2,1)S(1...) fusion(bf16[1,32,120,128]{3,2,1,0:T(8,128)(2,1)} %param.7), kind=kLoop, calls=%fused_computation.144 | loop fusion | bytes 8847360 | tf_op jit(solution)/shard_map/slice | solution.py:32
  19.3 16.0 %copy.215 = bf16[1,3840,128]{2,0,1:T(2,128)(2,1)} copy(bf16[1,3840,128]{2,1,0:T(8,128)(2,1)S(1)} %fusion.41) | data formatting | bytes 1966080 | tf_op jit(solution)/shard_map/convert_element_type | solution.py:120
  35.9 22.2 %reduce.4 = bf16[3840,128]{1,0:T(8,128)(2,1)S(1)} reduce(bf16[3840,1,128]{2,1,0:T(2,128)(2,1)} %bitcast.386, bf16[]{:T(256)} %broadcast.145), dimensions={1}, to_apply=%bitcast.378.reduce_sub_computation | reduce | bytes 1966082
  59.4 11.1 %all-to-all-start = ((bf16[128,2,1920]{2,1,0:T(2,128)(2,1)}), bf16[128,2,1920]{2,1,0:T(2,128)(2,1)S(1)}, u32[]{:S(2)}, u32[]{:S(2)}) async-start(bf16[128,2,1920]{2,1,0:T(2,128)(2,1)} %reshape.558), calls=%async_computation | async-start | bytes 1966080 | tf_op jit(solution)/shard_map/all_to_all | solution.py:106
  79.1 9.9 %copy.214 = bf16[1,3840,128]{2,0,1:T(2,128)(2,1)} copy(bf16[1,3840,128]{2,1,0:T(8,128)(2,1)} %bitcast.404) | data formatting | bytes 1966080 | tf_op jit(solution)/shard_map/reshape | solution.py:121
  89.0 23.1 %reduce.5 = bf16[3840,128]{1,0:T(8,128)(2,1)} reduce(bf16[3840,1,128]{2,1,0:T(2,128)(2,1)} %bitcast.387, bf16[]{:T(256)} %broadcast.145), dimensions={1}, to_apply=%bitcast.377.reduce_sub_computation | reduce | bytes 1966082
  112.1 3.0 reshape.560
  118.4 10.4 %all-to-all-start.2 = ((bf16[128,2,1920]{2,1,0:T(2,128)(2,1)}), bf16[128,2,1920]{2,1,0:T(2,128)(2,1)}, u32[]{:S(2)}, u32[]{:S(2)}) async-start(bf16[128,2,1920]{2,1,0:T(2,128)(2,1)} %reshape.560), calls=%async_computation.2 | async-start | bytes 1966080 | tf_op jit(solution)/shard_map/all_to_all | solution.py:123
  129.7 17.4 %bitcast_reduce_fusion.1 = bf16[3840,128]{1,0:T(8,128)(2,1)} fusion(bf16[3840,1,128]{2,1,0:T(2,128)(2,1)S(1)} %reshape.559), kind=kLoop, calls=%fused_computation.264 | loop fusion | bytes 1966080 | tf_op jit(solution)/shard_map/all_to_all | solution.py:106
  150.1 5.6 pad_dynamic-slice_fusion.12
  157.7 2.2 reshape.489
  159.9 2.7 copy.126
  162.6 2.2 reshape.486
  166.7 2.2 reshape.488
  171.0 2.5 reshape.485
  178.9 2.6 multiply_convert_fusion.11
  182.9 2.6 reshape.490
  185.5 2.3 copy.130
  188.4 3.5 pad_dynamic-slice_fusion.8
  191.9 2.7 copy.134
  194.6 2.2 reshape.494
  196.8 2.0 copy.132
  198.8 2.2 reshape.492
  204.3 2.0 copy.131
  206.3 2.2 reshape.491
  218.5 4.1 reshape.561
  222.7 17.5 %bitcast_reduce_fusion = bf16[3840,128]{1,0:T(8,128)(2,1)} fusion(bf16[3840,1,128]{2,1,0:T(2,128)(2,1)S(1)} %reshape.561), kind=kLoop, calls=%fused_computation.263 | loop fusion | bytes 1966080 | tf_op jit(solution)/shard_map/all_to_all | solution.py:123
  240.2 2.2 dot_general.217
  244.1 5.1 multiply_convert_fusion
  249.2 2.6 reshape.502
  251.8 2.9 copy.140
  254.7 2.9 copy.136
  257.7 4.2 multiply_convert_fusion.9
  262.9 3.2 pad_dynamic-slice_fusion.4
  266.1 2.7 copy.144
  268.8 2.2 reshape.504
  271.0 2.7 copy.142
  273.7 2.2 reshape.501
  275.8 2.2 copy.143
  279.4 2.7 copy.141
  282.1 2.2 reshape.500
  291.6 3.2 multiply_convert_fusion.6
  294.7 2.6 reshape.505
  297.4 2.9 copy.146
  300.3 2.9 multiply_convert_fusion.7
  304.2 3.5 pad_dynamic-slice_fusion
  310.5 2.3 reshape.531
  312.8 2.4 convolution_bitcast_fusion
  321.8 2.0 copy.148
  337.6 10.4 %all-to-all-start.3 = ((bf16[128,30,128]{2,1,0:T(8,128)(2,1)}), bf16[128,30,128]{2,1,0:T(8,128)(2,1)}, u32[]{:S(2)}, u32[]{:S(2)}) async-start(bf16[128,30,128]{2,1,0:T(8,128)(2,1)} %convert_element_type.196), calls=%async_computation.3 | async-start | bytes 2097152 | tf_op jit(solution)/shard_map/all_to_all | solution.py:110
  348.7 2.7 copy.137
  351.4 2.4 fusion.10
  357.8 8.0 %all-to-all-done.3 = bf16[128,30,128]{2,1,0:T(8,128)(2,1)} async-done(((bf16[128,30,128]{2,1,0:T(8,128)(2,1)}), bf16[128,30,128]{2,1,0:T(8,128)(2,1)}, u32[]{:S(2)}, u32[]{:S(2)}) %all-to-all-start.3) | async-done | bytes 983072 | tf_op jit(solution)/shard_map/all_to_all | solution.py:110
  365.8 5.8 all-to-all-start.1
  371.6 2.4 copy.151
  378.3 3.2 multiply_convert_fusion.3
  381.6 2.0 copy.156
  384.8 2.4 fusion.21
  396.4 2.3 multiply_convert_fusion.5
  398.7 3.7 pad_slice_fusion
  406.5 2.3 convolution_add_fusion.7
  418.3 127.8 %all-reduce.12.cloned.1.call-done = (f32[9,128,128]{2,1,0:T(8,128)}, f32[2,5,128,128]{3,2,1,0:T(8,128)}, f32[2,128,128]{2,1,0:T(8,128)}) async-done(((f32[9,128,128]{2,1,0:T(8,128)}, f32[2,5,128,128]{3,2,1,0:T(8,128)}, f32[2,128,128]{2,1,0:T(8,128)}), (f32[9,128,128]{2,1,0:T(8,128)}, f32[2,5,128,128]{3,2,1,0:T(8,128)}, f32[2,128,128]{2,1,0:T(8,128)})) %all-reduce.12.cloned.1.call-update) | async-done | bytes 1376272 | tf_op jit(solution)/shard_map/psum | solution.py:181
  551.6 136.0 %all-reduce.10.cloned.1.call-done = bf16[3840,128]{1,0:T(8,128)(2,1)} async-done(((bf16[3840,128]{1,0:T(8,128)(2,1)}), bf16[3840,128]{1,0:T(8,128)(2,1)}) %all-reduce.10.cloned.1.call-update) | async-done | bytes 983056 | tf_op jit(solution)/shard_map/psum | solution.py:12
  687.5 2.5 fusion
  (226 shorter events, 115.2 us)
Async XLA Ops:
  7.2 7.2 %copy-start.47 = (bf16[9,128,128]{2,1,0:T(8,128)(2,1)S(1)}, bf16[9,128,128]{2,1,0:T(8,128)(2,1)}, u32[]{:S(2)}) copy-start(bf16[9,128,128]{2,1,0:T(8,128)(2,1)} %param.8) | copy-start | bytes 884740
  15.6 1.2 copy-start.8
  18.8 58.8 %copy-start = (f32[3840,128]{1,0:T(8,128)}, f32[3840,128]{1,0:T(8,128)S(1)}, u32[]{:S(2)}) copy-start(f32[3840,128]{1,0:T(8,128)S(1)} %convolution_add_fusion.25) | copy-start | bytes 5898244
  58.2 12.4 %copy-start.57 = (s32[2]{0:T(128)S(1)}, s32[2]{0:T(128)}, u32[]{:S(2)}) copy-start(s32[2]{0:T(128)} %param.12) | copy-start | bytes 28
  59.4 59.0 %all-to-all-start = ((bf16[128,2,1920]{2,1,0:T(2,128)(2,1)}), bf16[128,2,1920]{2,1,0:T(2,128)(2,1)S(1)}, u32[]{:S(2)}, u32[]{:S(2)}) async-start(bf16[128,2,1920]{2,1,0:T(2,128)(2,1)} %reshape.558), calls=%async_computation | async-start | bytes 1966080 | tf_op jit(solution)/shard_map/all_to_all | solution.py:106
  89.0 26.2 %copy-start.23 = (f32[128,30,128]{2,1,0:T(8,128)S(1)}, f32[128,30,128]{2,1,0:T(8,128)}, u32[]{:S(2)}) copy-start(f32[128,30,128]{2,1,0:T(8,128)} %reshape.520) | copy-start | bytes 5898244
  115.2 1.9 copy-start.58
  118.4 100.1 %all-to-all-start.2 = ((bf16[128,2,1920]{2,1,0:T(2,128)(2,1)}), bf16[128,2,1920]{2,1,0:T(2,128)(2,1)}, u32[]{:S(2)}, u32[]{:S(2)}) async-start(bf16[128,2,1920]{2,1,0:T(2,128)(2,1)} %reshape.560), calls=%async_computation.2 | async-start | bytes 1966080 | tf_op jit(solution)/shard_map/all_to_all | solution.py:123
  129.7 46.6 %copy-start.6 = (bf16[3840,1,128]{2,1,0:T(2,128)(2,1)}, bf16[3840,1,128]{2,1,0:T(2,128)(2,1)S(1)}, u32[]{:S(2)}) copy-start(bf16[3840,1,128]{2,1,0:T(2,128)(2,1)S(1)} %reshape.559) | copy-start | bytes 2949124
  155.7 4.2 copy-start.10
  159.9 4.9 copy-start.12
  166.7 2.2 copy-start.15
  173.5 1.7 copy-start.37
  176.4 1.3 copy-start.34
  177.6 1.3 copy-start.51
  181.5 1.3 copy-start.29
  187.8 4.0 copy-start.2
  191.9 4.9 copy-start.19
  196.8 4.1 copy-start.17
  200.9 3.4 copy-start.21
  208.5 1.7 copy-start.38
  210.2 1.3 copy-start.30
  212.6 1.3 copy-start.33
  215.0 2.0 copy-start.3
  222.7 19.7 %copy-start.24 = (bf16[3840,1,128]{2,1,0:T(2,128)(2,1)}, bf16[3840,1,128]{2,1,0:T(2,128)(2,1)S(1)}, u32[]{:S(2)}) copy-start(bf16[3840,1,128]{2,1,0:T(2,128)(2,1)S(1)} %reshape.561) | copy-start | bytes 2949124
  240.2 3.6 copy-start.56
  257.7 4.2 copy-start.22
  284.3 1.7 copy-start.35
  286.0 1.6 copy-start.4
  286.0 2.1 copy-start.46
  289.7 1.6 copy-start.44
  289.8 1.8 copy-start.50
  304.2 3.5 copy-start.5
  304.2 3.5 copy-start.25
  307.7 1.2 copy-start.52
  310.5 4.8 copy-start.20
  312.8 2.5 copy-start.53
  312.8 2.9 copy-start.48
  312.8 2.9 copy-start.59
  315.3 1.3 copy-start.18
  315.7 1.3 copy-start.16
  316.6 1.3 copy-start.14
  317.0 1.9 copy-start.40
  321.8 3.2 copy-start.39
  329.7 1.7 copy-start.36
  331.5 1.3 copy-start.49
  333.9 1.3 copy-start.43
  337.6 13.8 %copy-start.7 = (bf16[3840,1,128]{2,1,0:T(2,128)(2,1)S(1)}, bf16[3840,1,128]{2,1,0:T(2,128)(2,1)}, u32[]{:S(2)}) copy-start(bf16[3840,1,128]{2,1,0:T(2,128)(2,1)} %copy-done.6) | copy-start | bytes 2949124
  337.6 28.2 %all-to-all-start.3 = ((bf16[128,30,128]{2,1,0:T(8,128)(2,1)}), bf16[128,30,128]{2,1,0:T(8,128)(2,1)}, u32[]{:S(2)}, u32[]{:S(2)}) async-start(bf16[128,30,128]{2,1,0:T(8,128)(2,1)} %convert_element_type.196), calls=%async_computation.3 | async-start | bytes 2097152 | tf_op jit(solution)/shard_map/all_to_all | solution.py:110
  351.4 2.4 copy-start.13
  351.4 3.5 copy-start.11
  353.8 2.1 copy-start.55
  365.8 38.3 %all-to-all-start.1 = ((bf16[128,30,128]{2,1,0:T(8,128)(2,1)}), bf16[128,30,128]{2,1,0:T(8,128)(2,1)}, u32[]{:S(2)}, u32[]{:S(2)}) async-start(bf16[128,30,128]{2,1,0:T(8,128)(2,1)} %copy.137), calls=%async_computation.1 | async-start | bytes 2097152 | tf_op jit(solution)/shard_map/all_to_all | solution.py:110
  371.6 174.5 %all-reduce.12.cloned.1.call-start = ((), (), s32[]{:S(2)}) async-start(), calls=%async_computation.5 | async-start | bytes 2752512 | tf_op jit(solution)/shard_map/psum | solution.py:181
  381.6 3.2 copy-start.9
  384.8 2.4 copy-start.41
  394.8 1.6 copy-start.1
  396.0 291.6 %all-reduce.10.cloned.1.call-start = ((), (), s32[]{:S(2)}) async-start(), calls=%async_computation.4 | async-start | bytes 1966080 | tf_op jit(solution)/shard_map/psum | solution.py:12
  406.5 2.4 copy-start.32
  408.9 1.2 copy-start.31
  410.1 1.6 copy-start.45
  411.7 1.2 copy-start.28
  412.9 1.2 copy-start.27
  414.1 1.2 copy-start.26
  (2 other events, 2.2 us)
Sparse Core Ops, SparseCore 0:
  396.1 149.9 all-reduce.11
  549.3 138.1 all-reduce.9
where the time goes:
time: 707 us; the launch traced here: 697 us
  waiting for transfers between devices  272 us (38%)
  local copies, waits for them, and re-layouts  221 us (31%)
  matrix products  74.7 us (11%)
  other arithmetic  69.4 us (10%)
  starting transfers between devices  37.8 us (5%)
  between operations  22.4 us (3%)
    psum x1, waiting for transfers between devices, from_root(): return lax.psum(jnp.where(mine, value, jnp.zeros_like(value)), axis)  136 us
    psum x1, waiting for transfers between devices, local(): lax.psum((grad_spatial, jnp.stack(tgrads), grad_uniting), ('seg', 'grp'))  128 us
    dynamic_slice x20, local copies, waits for them, and re-layouts, shifted(): return lax.dynamic_slice_in_dim(padded, start, values.shape[0], 0)  50.3 us
    unnamed x2, other arithmetic  45.3 us
    dot_general x21, matrix products, inner(): lax.dot_general(left, right, (((0,), (0,)), ((), ())), preferred_element_...  24 us
    all_to_all x3, local copies, waits for them, and re-layouts, to_pixels(): lax.all_to_all(flat, ('seg', 'grp'), split_axis=1, concat_axis=0, tiled=T...  20.4 us
    unnamed x125, local copies, waits for them, and re-layouts  18.4 us
    all_to_all x1, local copies, waits for them, and re-layouts, local(): lax.all_to_all(cot_local, ('seg', 'grp'), split_axis=1, concat_axis=0, ti...  17.5 us
  transfers between devices with their start and end apart: 6, of which 3 were waited for; matrix products, arithmetic and copies ran while one was open for 27% of the time, Pallas kernels for 0%

commit v1 on v0

--- a/solution.py
+++ b/solution.py
@@ -9,7 +9,7 @@
 
 def from_root(value, axis, root):
     mine = lax.axis_index(axis) == root
-    return lax.psum(jnp.where(mine, value, jnp.zeros_like(value)), axis)
+    return jnp.sum(lax.all_gather(jnp.where(mine, value, jnp.zeros_like(value)), axis), axis=0)
 
 
 def silu_grad(value):

time: 707 us -> 670 us (0.948)
  waiting for transfers between devices: 272 us -> 181 us
  local copies, waits for them, and re-layouts: 221 us -> 249 us
  matrix products: 74.7 us -> 84.5 us
  other arithmetic: 69.4 us -> 78.8 us
    psum x1 -> x0, waiting for transfers between devices: 136 us -> none  [from_root(): return lax.psum(jnp.where(mine, value, jnp.zeros_like(value)), axis)]
    psum x1, waiting for transfers between devices: 128 us -> 181 us  [local(): lax.psum((grad_spatial, jnp.stack(tgrads), grad_uniting), ('seg', 'grp'))]
    reduce_sum x0 -> x1, other arithmetic: none -> 8.64 us  [from_root(): jnp.sum(lax.all_gather(jnp.where(mine, value, jnp.zeros_like(value)), axi...]
    dynamic_slice x20, local copies, waits for them, and re-layouts: 50.3 us -> 58.5 us  [shifted(): return lax.dynamic_slice_in_dim(padded, start, values.shape[0], 0)]
    dot_general x10, matrix products: 15.7 us -> 23.8 us  [temporal_back(): jnp.dot(piece, kernel[tap].T, preferred_element_type=jnp.float32)]
    all_to_all x2, waiting for transfers between devices: 8.03 us -> 0.01 us  [to_frames(): lax.all_to_all(blocks, ('seg', 'grp'), split_axis=0, concat_axis=1, tiled...]
    unnamed x125 -> x85, local copies, waits for them, and re-layouts: 18.4 us -> 19.5 us
  transfers between devices with their start and end apart: 6 -> 6, of which waited for: 3 -> 1; matrix products, arithmetic and copies ran while one was open for 27% -> 33% of each run, Pallas kernels for 0% -> 0%
where the time goes in v1:
time: 670 us; the launch traced here: 659 us
  local copies, waits for them, and re-layouts  249 us (37%)
  waiting for transfers between devices  181 us (27%)
  matrix products  84.5 us (13%)
  other arithmetic  78.8 us (12%)
  starting transfers between devices  41.7 us (6%)
  between operations  23.5 us (4%)
    psum x1, waiting for transfers between devices, local(): lax.psum((grad_spatial, jnp.stack(tgrads), grad_uniting), ('seg', 'grp'))  181 us
    dynamic_slice x20, local copies, waits for them, and re-layouts, shifted(): return lax.dynamic_slice_in_dim(padded, start, values.shape[0], 0)  58.5 us
    unnamed x2, other arithmetic  45.2 us
    dot_general x21, matrix products, inner(): lax.dot_general(left, right, (((0,), (0,)), ((), ())), preferred_element_...  24.4 us
    dot_general x10, matrix products, temporal_back(): jnp.dot(piece, kernel[tap].T, preferred_element_type=jnp.float32)  23.8 us
    all_to_all x3, local copies, waits for them, and re-layouts, to_pixels(): lax.all_to_all(flat, ('seg', 'grp'), split_axis=1, concat_axis=0, tiled=T...  21.4 us
    all_to_all x2, starting transfers between devices, to_frames(): lax.all_to_all(blocks, ('seg', 'grp'), split_axis=0, concat_axis=1, tiled...  20.1 us
    unnamed x85, local copies, waits for them, and re-layouts  19.5 us
  transfers between devices with their start and end apart: 6, of which 1 were waited for; matrix products, arithmetic and copies ran while one was open for 33% of the time, Pallas kernels for 0%

profile of v1, /device:TPU:0, one launch (start us, length us, event | category | flops | bytes accessed | tf_op | source)
XLA Modules:
  0.0 659.1 jit_solution(5562274995653732031)
XLA Ops:
  8.0 7.3 %pad_slice_fusion.8 = (bf16[1,32,120,128]{3,2,1,0:T(8,128)(2,1)S(1)}, bf16[1,32,120,128]{3,2,1,0:T(8,128)(2,1)S(1)}, bf16[1,32,120,128]{3,2,1,0:T(8,128)(2,1)S(1...) fusion(bf16[1,32,120,128]{3,2,1,0:T(8,128)(2,1)} %param.7), kind=kLoop, calls=%fused_computation.144 | loop fusion | bytes 8847360 | tf_op jit(solution)/shard_map/slice | solution.py:32
  20.3 16.0 %copy.216 = bf16[1,3840,128]{2,0,1:T(2,128)(2,1)} copy(bf16[1,3840,128]{2,1,0:T(8,128)(2,1)S(1)} %fusion.41) | data formatting | bytes 1966080 | tf_op jit(solution)/shard_map/convert_element_type | solution.py:120
  36.9 22.2 %reduce.5 = bf16[3840,128]{1,0:T(8,128)(2,1)S(1)} reduce(bf16[3840,1,128]{2,1,0:T(2,128)(2,1)} %bitcast.386, bf16[]{:T(256)} %broadcast.163), dimensions={1}, to_apply=%bitcast.378.reduce_sub_computation | reduce | bytes 1966082
  60.4 11.1 %all-to-all-start = ((bf16[128,2,1920]{2,1,0:T(2,128)(2,1)}), bf16[128,2,1920]{2,1,0:T(2,128)(2,1)S(1)}, u32[]{:S(2)}, u32[]{:S(2)}) async-start(bf16[128,2,1920]{2,1,0:T(2,128)(2,1)} %reshape.571), calls=%async_computation | async-start | bytes 1966080 | tf_op jit(solution)/shard_map/all_to_all | solution.py:106
  80.1 9.9 %copy.215 = bf16[1,3840,128]{2,0,1:T(2,128)(2,1)} copy(bf16[1,3840,128]{2,1,0:T(8,128)(2,1)} %bitcast.404) | data formatting | bytes 1966080 | tf_op jit(solution)/shard_map/reshape | solution.py:121
  89.9 23.0 %reduce.6 = bf16[3840,128]{1,0:T(8,128)(2,1)} reduce(bf16[3840,1,128]{2,1,0:T(2,128)(2,1)} %bitcast.387, bf16[]{:T(256)} %broadcast.163), dimensions={1}, to_apply=%bitcast.377.reduce_sub_computation | reduce | bytes 1966082
  112.9 3.1 reshape.573
  116.0 2.9 copy.155
  119.0 10.4 %all-to-all-start.2 = ((bf16[128,2,1920]{2,1,0:T(2,128)(2,1)}), bf16[128,2,1920]{2,1,0:T(2,128)(2,1)}, u32[]{:S(2)}, u32[]{:S(2)}) async-start(bf16[128,2,1920]{2,1,0:T(2,128)(2,1)} %reshape.573), calls=%async_computation.2 | async-start | bytes 1966080 | tf_op jit(solution)/shard_map/all_to_all | solution.py:123
  129.5 3.3 reshape.572
  132.8 18.4 %bitcast_reduce_fusion.1 = bf16[3840,128]{1,0:T(8,128)(2,1)} fusion(bf16[3840,1,128]{2,1,0:T(2,128)(2,1)} %reshape.572), kind=kLoop, calls=%fused_computation.264 | loop fusion | bytes 1966080 | tf_op jit(solution)/shard_map/all_to_all | solution.py:106
  154.2 5.5 pad_dynamic-slice_fusion.12
  159.7 3.0 copy.126
  164.9 2.6 copy.127
  169.7 2.6 copy.128
  184.1 3.0 multiply_convert_fusion.11
  187.0 3.0 reshape.503
  190.0 2.9 copy.131
  195.0 3.2 pad_dynamic-slice_fusion.8
  198.2 3.0 copy.132
  203.4 2.9 fusion.62
  206.3 2.7 copy.133
  211.1 2.7 copy.134
  226.6 2.6 reshape.542
  229.2 2.7 reshape.508
  231.9 5.6 reshape.574
  237.5 18.6 %bitcast_reduce_fusion = bf16[3840,128]{1,0:T(8,128)(2,1)} fusion(bf16[3840,1,128]{2,1,0:T(2,128)(2,1)} %reshape.574), kind=kLoop, calls=%fused_computation.263 | loop fusion | bytes 1966080 | tf_op jit(solution)/shard_map/all_to_all | solution.py:123
  257.9 4.7 multiply_convert_fusion
  262.6 2.6 reshape.515
  265.3 3.0 copy.141
  268.3 2.9 copy.137
  271.2 4.1 multiply_convert_fusion.9
  275.3 3.6 pad_dynamic-slice_fusion.4
  279.9 2.7 copy.142
  284.8 2.9 fusion.60
  287.7 2.7 copy.143
  292.6 3.1 copy.144
  297.8 2.7 copy.145
  309.3 3.1 multiply_convert_fusion.6
  312.5 2.6 reshape.518
  315.1 2.9 copy.147
  318.1 3.0 multiply_convert_fusion.7
  321.5 3.7 pad_dynamic-slice_fusion
  329.5 2.7 copy.148
  334.3 2.9 fusion.72
  337.2 2.7 copy.149
  344.4 2.5 convolution_add_fusion.10
  346.9 2.7 copy.150
  351.7 2.8 copy.151
  363.4 10.4 %all-to-all-start.3 = ((bf16[128,30,128]{2,1,0:T(8,128)(2,1)}), bf16[128,30,128]{2,1,0:T(8,128)(2,1)}, u32[]{:S(2)}, u32[]{:S(2)}) async-start(bf16[128,30,128]{2,1,0:T(8,128)(2,1)} %convert_element_type.198), calls=%async_computation.3 | async-start | bytes 2097152 | tf_op jit(solution)/shard_map/all_to_all | solution.py:110
  378.8 3.0 convolution_bitcast_fusion.1
  385.1 2.7 copy.138
  387.8 3.1 fusion.5
  394.9 9.7 %all-to-all-start.1 = ((bf16[128,30,128]{2,1,0:T(8,128)(2,1)}), bf16[128,30,128]{2,1,0:T(8,128)(2,1)S(1)}, u32[]{:S(2)}, u32[]{:S(2)}) async-start(bf16[128,30,128]{2,1,0:T(8,128)(2,1)} %copy.138), calls=%async_computation.1 | async-start | bytes 2097152 | tf_op jit(solution)/shard_map/all_to_all | solution.py:110
  404.6 2.6 copy.152
  407.2 3.5 multiply_convert_fusion.3
  410.7 2.7 copy.157
  415.5 2.7 fusion.21
  431.8 2.8 copy.153
  434.6 2.6 reshape.545
  437.3 2.6 reshape.546
  441.1 2.5 multiply_convert_fusion.5
  454.8 181.1 %all-reduce.9.cloned.1.call-done = (f32[9,128,128]{2,1,0:T(8,128)}, f32[2,5,128,128]{3,2,1,0:T(8,128)}, f32[2,128,128]{2,1,0:T(8,128)}) async-done(((f32[9,128,128]{2,1,0:T(8,128)}, f32[2,5,128,128]{3,2,1,0:T(8,128)}, f32[2,128,128]{2,1,0:T(8,128)}), (f32[9,128,128]{2,1,0:T(8,128)}, f32[2,5,128,128]{3,2,1,0:T(8,128)}, f32[2,128,128]{2,1,0:T(8,128)})) %all-reduce.9.cloned.1.call-update) | async-done | bytes 1376272 | tf_op jit(solution)/shard_map/psum | solution.py:181
  641.4 8.6 %reduce_sum.21 = bf16[3840,128]{1,0:T(8,128)(2,1)S(1)} reduce(bf16[16,3840,128]{2,1,0:T(8,128)(2,1)} %all-gather.2.cloned.1.call-done, bf16[]{:T(256)} %constant.79.clone.1), dimensions={0}, to_apply=%region_0.1 | reduce | flops 7372800 | bytes 16711682 | tf_op jit(solution)/shard_map/reduce_sum | solution.py:12
  (188 shorter events, 134.0 us)
Async XLA Ops:
  8.0 7.3 %copy-start.29 = (bf16[9,128,128]{2,1,0:T(8,128)(2,1)S(1)}, bf16[9,128,128]{2,1,0:T(8,128)(2,1)}, u32[]{:S(2)}) copy-start(bf16[9,128,128]{2,1,0:T(8,128)(2,1)} %param.8) | copy-start | bytes 884740
  16.5 1.2 copy-start.3
  59.1 12.4 %copy-start.38 = (s32[2]{0:T(128)S(1)}, s32[2]{0:T(128)}, u32[]{:S(2)}) copy-start(s32[2]{0:T(128)} %param.12) | copy-start | bytes 28
  60.4 58.7 %all-to-all-start = ((bf16[128,2,1920]{2,1,0:T(2,128)(2,1)}), bf16[128,2,1920]{2,1,0:T(2,128)(2,1)S(1)}, u32[]{:S(2)}, u32[]{:S(2)}) async-start(bf16[128,2,1920]{2,1,0:T(2,128)(2,1)} %reshape.571), calls=%async_computation | async-start | bytes 1966080 | tf_op jit(solution)/shard_map/all_to_all | solution.py:106
  116.0 2.9 copy-start.39
  119.0 112.9 %all-to-all-start.2 = ((bf16[128,2,1920]{2,1,0:T(2,128)(2,1)}), bf16[128,2,1920]{2,1,0:T(2,128)(2,1)}, u32[]{:S(2)}, u32[]{:S(2)}) async-start(bf16[128,2,1920]{2,1,0:T(2,128)(2,1)} %reshape.573), calls=%async_computation.2 | async-start | bytes 1966080 | tf_op jit(solution)/shard_map/all_to_all | solution.py:123
  159.7 14.8 %copy-start.8 = (bf16[128,30,128]{0,2,1:T(8,128)(2,1)}, bf16[128,30,128]{0,2,1:T(8,128)(2,1)S(1)}, u32[]{:S(2)}) copy-start(bf16[128,30,128]{0,2,1:T(8,128)(2,1)S(1)} %get-tuple-element.32) | copy-start | bytes 2949124
  176.5 2.2 copy-start.24
  178.7 1.2 copy-start.21
  180.0 1.6 copy-start.1
  181.5 1.3 copy-start.18
  182.8 1.3 copy-start.32
  198.2 17.7 %copy-start.5 = (bf16[128,30,128]{0,2,1:T(8,128)(2,1)}, bf16[128,30,128]{0,2,1:T(8,128)(2,1)S(1)}, u32[]{:S(2)}) copy-start(bf16[128,30,128]{0,2,1:T(8,128)(2,1)S(1)} %get-tuple-element.28) | copy-start | bytes 2949124
  219.3 2.4 copy-start.17
  221.7 1.3 copy-start.20
  256.1 1.6 copy-start.37
  275.3 3.6 copy-start.14
  302.8 2.4 copy-start
  302.8 3.0 copy-start.27
  305.8 1.7 copy-start.19
  307.5 1.6 copy-start.26
  307.5 1.8 copy-start.33
  318.1 3.0 copy-start.12
  321.4 3.7 copy-start.11
  321.5 4.1 copy-start.30
  325.1 1.5 copy-start.2
  325.1 2.0 copy-start.10
  326.7 1.3 copy-start.9
  327.2 1.3 copy-start.13
  328.4 1.1 copy-start.35
  342.0 2.4 copy-start.31
  356.7 2.4 copy-start.25
  363.4 31.4 %all-to-all-start.3 = ((bf16[128,30,128]{2,1,0:T(8,128)(2,1)}), bf16[128,30,128]{2,1,0:T(8,128)(2,1)}, u32[]{:S(2)}, u32[]{:S(2)}) async-start(bf16[128,30,128]{2,1,0:T(8,128)(2,1)} %convert_element_type.198), calls=%async_computation.3 | async-start | bytes 2097152 | tf_op jit(solution)/shard_map/all_to_all | solution.py:110
  378.8 3.0 copy-start.15
  378.8 3.0 copy-start.34
  387.8 3.1 copy-start.7
  387.8 4.2 copy-start.6
  390.9 2.1 copy-start.36
  394.9 33.5 %all-to-all-start.1 = ((bf16[128,30,128]{2,1,0:T(8,128)(2,1)}), bf16[128,30,128]{2,1,0:T(8,128)(2,1)S(1)}, u32[]{:S(2)}, u32[]{:S(2)}) async-start(bf16[128,30,128]{2,1,0:T(8,128)(2,1)} %copy.138), calls=%async_computation.1 | async-start | bytes 2097152 | tf_op jit(solution)/shard_map/all_to_all | solution.py:110
  404.6 231.3 %all-reduce.9.cloned.1.call-start = ((), (), s32[]{:S(2)}) async-start(), calls=%async_computation.5 | async-start | bytes 2752512 | tf_op jit(solution)/shard_map/psum | solution.py:181
  415.5 2.7 copy-start.4
  415.5 2.7 copy-start.22
  427.0 214.3 %all-gather.2.cloned.1.call-start = ((), (), s32[]{:S(2)}) async-start(), calls=%async_computation.4 | async-start | bytes 16711680 | tf_op jit(solution)/shard_map/all_gather | solution.py:12
  446.0 1.2 copy-start.23
  449.8 1.5 copy-start.28
  641.4 8.7 %copy-start.16 = (f32[3840,128]{1,0:T(8,128)S(1)}, f32[3840,128]{1,0:T(8,128)}, u32[]{:S(2)}) copy-start(f32[3840,128]{1,0:T(8,128)} %fusion.50) | copy-start | bytes 5898244
Sparse Core Ops, SparseCore 0:
  427.2 208.6 all-reduce.8
Sparse Core Ops, SparseCore 1:
  431.9 106.7 all-gather.1
